TPU v7x, 512 devices: a whole 4x4x16 slice. The times are simulated.
512 devices in a mesh: row: 16 (over y_hi, x, core), col: 32 (over y_lo, z).
Axes of the slice: x: 4, y: 4 (y_hi: 2, y_lo: 2; y = y_hi * 2 + y_lo), z: 16, core: 2. Of those that a mesh axis runs over, the one named last changes fastest.
Arguments:
- inputs: bfloat16 [256, 512, 256], P('row', 'col'), may hold values from -6 to 6
- stored: bfloat16 [256, 512, 256], P('row', 'col'), may hold values from -6 to 6
- upstream: bfloat16 [256, 512, 256], P('row', 'col'), may hold values from -6 to 6
- weight_in: bfloat16 [256, 1024], replicated, may hold values from -0.375 to 0.375
- weight_out: bfloat16 [1024, 256], replicated, may hold values from -0.1875 to 0.1875
- kernel: bfloat16 [27, 27, 256], replicated, may hold values from -0.21875 to 0.21875
Outputs:
- grad_inputs: bfloat16 [256, 512, 256], P('row', 'col')
- grad_weight_in: bfloat16 [256, 1024], replicated
- grad_weight_out: bfloat16 [1024, 256], replicated
- grad_kernel: bfloat16 [27, 27, 256], replicated
All inputs are finite; a program needn't handle non-finite values.
Results may differ from a plain program's by a relative error of at most 0.0052.
Values may be sent and summed in bfloat16 or wider, within the bound.
No kernel may reach another device: no remote copies, remote signals or barrier semaphores. Data moves between devices by JAX's collectives and lax.ppermute only.
A program may use at most 64 MiB of HBM per device.

v0:
```python
import math
import jax
import jax.numpy as jnp
from jax import lax
from jax.sharding import PartitionSpec as P

KS = 27
gelu_coef = 0.044715
root_coef = math.sqrt(2.0 / math.pi)


def padded_2(block, sides, width):
    for axis, dim in sides:
        count = lax.axis_size(axis)
        forward = [(i, i + 1) for i in range(count - 1)]
        backward = [(target, source) for source, target in forward]
        low = lax.ppermute(
            lax.slice_in_dim(block, block.shape[dim] - width, None, axis=dim), axis, forward
        )
        high = lax.ppermute(lax.slice_in_dim(block, 0, width, axis=dim), axis, backward)
        block = jnp.concatenate([low, block, high], axis=dim)
    return block


def gelu_parts(values):
    tanh_part = jnp.tanh(root_coef * (values + gelu_coef * values * values * values))
    result = 0.5 * values * (1.0 + tanh_part)
    slopes = 0.5 * (1.0 + tanh_part) + 0.5 * values * (1.0 - tanh_part * tanh_part) * root_coef * (
        1.0 + 3.0 * gelu_coef * values * values
    )
    return (result, slopes)


def per_device(inputs, stored, upstream, weight_in, weight_out, kernel):
    tile_rows, tile_cols, channels = stored.shape
    radius = KS // 2
    padded_in = padded_2(inputs, (("row", 0), ("col", 1)), radius)
    flat_z = stored.reshape(tile_rows * tile_cols, channels)
    flat_g = upstream.reshape(tile_rows * tile_cols, channels)
    hidden = jnp.dot(flat_z, weight_in, preferred_element_type=jnp.float32)
    values, slopes = gelu_parts(hidden)
    active = values.astype(jnp.bfloat16)
    back_proj = jnp.einsum("nc,fc->nf", flat_g, weight_out, preferred_element_type=jnp.float32)
    grad_hidden = (back_proj * slopes).astype(jnp.bfloat16)
    grad_flat = (
        flat_g.astype(jnp.float32)
        + jnp.einsum("nf,cf->nc", grad_hidden, weight_in, preferred_element_type=jnp.float32)
    ).astype(jnp.bfloat16)
    sum_in = jnp.einsum("nc,nf->cf", flat_z, grad_hidden, preferred_element_type=jnp.float32)
    sum_out = jnp.einsum("nf,nc->fc", active, flat_g, preferred_element_type=jnp.float32)
    grad_mid = grad_flat.reshape(tile_rows, tile_cols, channels)
    padded = padded_2(grad_mid, (("row", 0), ("col", 1)), radius)
    kernel_wide = kernel.astype(jnp.float32)

    def sweep(row_off, state_pair):
        accumulated, kernel_sums = state_pair
        slab_rows = lax.dynamic_slice_in_dim(padded, 2 * radius - row_off, tile_rows, 0)
        tap_row = lax.dynamic_index_in_dim(kernel_wide, row_off, 0, keepdims=False)
        tap_sums = []
        source_rows = lax.dynamic_slice_in_dim(padded_in, row_off, tile_rows, 0)
        for offset in range(KS):
            shifted = slab_rows[:, 2 * radius - offset : 2 * radius - offset + tile_cols].astype(
                jnp.float32
            )
            accumulated = accumulated + tap_row[offset] * shifted
            tap_sums.append(
                jnp.sum(
                    source_rows[:, offset : offset + tile_cols].astype(jnp.float32)
                    * grad_mid.astype(jnp.float32),
                    axis=(0, 1),
                )
            )
        kernel_sums = lax.dynamic_update_index_in_dim(kernel_sums, jnp.stack(tap_sums), row_off, 0)
        return (accumulated, kernel_sums)

    start = (
        jnp.zeros((tile_rows, tile_cols, channels), jnp.float32),
        jnp.zeros((KS, KS, channels), jnp.float32),
    )
    accumulated, kernel_sums = lax.fori_loop(0, KS, sweep, start)
    grad_inputs = (grad_mid.astype(jnp.float32) + accumulated).astype(jnp.bfloat16)
    devices_all = lax.axis_size("row") * lax.axis_size("col")
    pixel_count = tile_rows * tile_cols * devices_all
    grad_scale = 1.0 / math.sqrt(pixel_count)
    total_in, total_out, total_kernel = lax.psum((sum_in, sum_out, kernel_sums), ("row", "col"))
    final_in = (total_in * grad_scale).astype(jnp.bfloat16)
    final_out = (total_out * grad_scale).astype(jnp.bfloat16)
    final_kernel = (total_kernel * grad_scale).astype(jnp.bfloat16)
    return (grad_inputs, final_in, final_out, final_kernel)


def solution(mesh):
    return jax.shard_map(
        per_device,
        mesh=mesh,
        in_specs=(
            P("row", "col", None),
            P("row", "col", None),
            P("row", "col", None),
            P(),
            P(),
            P(),
        ),
        out_specs=(P("row", "col", None), P(), P(), P()),
        check_vma=False,
    )
```

profile of v0, /device:TPU:8, one launch (start us, length us, event | category | flops | bytes accessed | tf_op | source)
XLA Modules:
  0.0 736.3 jit_solution(15265155077819901932)
XLA Ops:
  9.6 3.0 collective-permute-start.4
  16.3 3.8 collective-permute-start
  23.0 4.0 collective-permute-start.6
  27.0 9.4 %collective-permute-start.7 = (bf16[42,13,256]{2,1,0:T(8,128)(2,1)S(1)}, bf16[42,13,256]{2,1,0:T(8,128)(2,1)S(1)}, u32[]{:S(2)}, u32[]{:S(2)}) collective-permute-start(bf16[42,13,256]{2,1,0:T(8,128)(2,1)S(1)} %get-tuple-element.283), channel_id=1, source_target_pairs={{1,0},{2,1},{3,2},{4,3},{5,4},{6,5},{7,6},{8,7},{9,8},{10,9},{11,1... | collective-permute-start | bytes 838664 | tf_op jit(solution)/shard_map/ppermute | solution.py:20
  38.5 6.0 collective-permute-start.3
  46.4 4.6 collective-permute-done.2
  53.4 179.6 %while.18 = (s32[]{:T(128)}, f32[16,16,256]{2,1,0:T(8,128)S(1)}, f32[27,27,256]{2,1,0:T(8,128)}, f32[27,27,256]{2,1,0:T(8,128)}, bf16[42,42,256]{2,1,0:T(8,128)(...) while((s32[]{:T(128)}, f32[16,16,256]{2,1,0:T(8,128)S(1)}, ...), condition=%wide.region_28.29_spmd.clone, body=%wide.region_0.28_spmd.clone.sunk | while | flops 10806561 | bytes 8091653 | solution.py:80
  57.4 2.1 multiply_add_fusion.3
  64.0 2.1 multiply_add_fusion.3
  70.6 2.1 multiply_add_fusion.3
  77.4 2.1 multiply_add_fusion.3
  84.1 2.1 multiply_add_fusion.3
  90.7 2.1 multiply_add_fusion.3
  97.4 2.1 multiply_add_fusion.3
  104.0 2.1 multiply_add_fusion.3
  110.6 2.1 multiply_add_fusion.3
  117.3 2.1 multiply_add_fusion.3
  123.9 2.1 multiply_add_fusion.3
  130.6 2.1 multiply_add_fusion.3
  137.2 2.1 multiply_add_fusion.3
  143.9 2.1 multiply_add_fusion.3
  150.5 2.1 multiply_add_fusion.3
  157.2 2.1 multiply_add_fusion.3
  163.8 2.1 multiply_add_fusion.3
  170.4 2.1 multiply_add_fusion.3
  183.7 2.1 multiply_add_fusion.3
  190.4 2.1 multiply_add_fusion.3
  197.0 2.1 multiply_add_fusion.3
  203.7 2.1 multiply_add_fusion.3
  210.3 2.1 multiply_add_fusion.3
  223.6 2.1 multiply_add_fusion.3
  233.7 491.6 %all-reduce.3.cloned.1.call-done = (f32[256,1024]{0,1:T(8,128)}, f32[1024,256]{1,0:T(8,128)}, f32[27,27,256]{2,1,0:T(8,128)}) async-done(((f32[256,1024]{0,1:T(8,128)}, f32[1024,256]{1,0:T(8,128)}, f32[27,27,256]{2,1,0:T(8,128)}), (f32[256,1024]{0,1:T(8,128)}, f32[1024,256]{1,0:T(8,128)}, f32[27,27,256]{2,1,0:T(8,128)})) %all-reduce.3.cloned.1.call-update) | async-done | bytes 2843664 | tf_op jit(solution)/shard_map/psum | solution.py:85
  (216 shorter events, 148.9 us)
Async XLA Ops:
  7.2 5.5 copy-start
  7.2 6.7 copy-start.7
  7.2 6.7 copy-start.6
  7.2 718.1 %all-reduce.3.cloned.1.call-start = ((), (), s32[]{:S(2)}) async-start(), calls=%async_computation | async-start | bytes 5963776 | tf_op jit(solution)/shard_map/psum | solution.py:85
  8.3 14.5 %collective-permute-start.5 = (bf16[13,16,256]{2,1,0:T(8,128)(2,1)S(1)}, bf16[13,16,256]{2,1,0:T(8,128)(2,1)S(1)}, u32[]{:S(2)}, u32[]{:S(2)}) collective-permute-start(bf16[13,16,256]{2,1,0:T(8,128)(2,1)S(1)} %get-tuple-element.286), channel_id=1, source_target_pairs={{32,0},{64,32},{96,64},{128,96},{160,128},{192,160},{224,192},{256... | collective-permute-start | bytes 319496 | tf_op jit(solution)/shard_map/ppermute | solution.py:20
  9.6 13.1 %collective-permute-start.4 = (bf16[13,16,256]{2,1,0:T(8,128)(2,1)S(1)}, bf16[13,16,256]{2,1,0:T(8,128)(2,1)S(1)}, u32[]{:S(2)}, u32[]{:S(2)}) collective-permute-start(bf16[13,16,256]{2,1,0:T(8,128)(2,1)S(1)} %get-tuple-element.287), channel_id=1, source_target_pairs={{0,32},{32,64},{64,96},{96,128},{128,160},{160,192},{192,224},{224... | collective-permute-start | bytes 319496 | tf_op jit(solution)/shard_map/ppermute | solution.py:17
  15.0 21.3 %collective-permute-start.1 = (bf16[13,16,256]{2,1,0:T(8,128)(2,1)S(1)}, bf16[13,16,256]{2,1,0:T(8,128)(2,1)S(1)}, u32[]{:S(2)}, u32[]{:S(2)}) collective-permute-start(bf16[13,16,256]{2,1,0:T(8,128)(2,1)S(1)} %bitcast.191), channel_id=1, source_target_pairs={{32,0},{64,32},{96,64},{128,96},{160,128},{192,160},{224,192},{256... | collective-permute-start | bytes 319496 | tf_op jit(solution)/shard_map/ppermute | solution.py:20
  16.3 5.4 copy-start.5
  16.3 20.0 %collective-permute-start = (bf16[13,16,256]{2,1,0:T(8,128)(2,1)S(1)}, bf16[13,16,256]{2,1,0:T(8,128)(2,1)S(1)}, u32[]{:S(2)}, u32[]{:S(2)}) collective-permute-start(bf16[13,16,256]{2,1,0:T(8,128)(2,1)S(1)} %bitcast.190), channel_id=1, source_target_pairs={{0,32},{32,64},{64,96},{96,128},{128,160},{160,192},{192,224},{224... | collective-permute-start | bytes 319496 | tf_op jit(solution)/shard_map/ppermute | solution.py:17
  21.7 1.0 copy-start.2
  23.0 21.6 %copy-start.4 = (bf16[16,16,256]{2,1,0:T(8,128)(2,1)S(1)}, bf16[16,16,256]{2,1,0:T(8,128)(2,1)}, u32[]{:S(2)}) copy-start(bf16[16,16,256]{2,1,0:T(8,128)(2,1)} %param.9) | copy-start | bytes 393220
  23.0 23.0 %collective-permute-start.6 = (bf16[42,13,256]{2,1,0:T(8,128)(2,1)S(1)}, bf16[42,13,256]{2,1,0:T(8,128)(2,1)S(1)}, u32[]{:S(2)}, u32[]{:S(2)}) collective-permute-start(bf16[42,13,256]{2,1,0:T(8,128)(2,1)S(1)} %get-tuple-element.282), channel_id=1, source_target_pairs={{0,1},{1,2},{2,3},{3,4},{4,5},{5,6},{6,7},{7,8},{8,9},{9,10},{10,1... | collective-permute-start | bytes 838664 | tf_op jit(solution)/shard_map/ppermute | solution.py:17
  27.0 19.0 %collective-permute-start.7 = (bf16[42,13,256]{2,1,0:T(8,128)(2,1)S(1)}, bf16[42,13,256]{2,1,0:T(8,128)(2,1)S(1)}, u32[]{:S(2)}, u32[]{:S(2)}) collective-permute-start(bf16[42,13,256]{2,1,0:T(8,128)(2,1)S(1)} %get-tuple-element.283), channel_id=1, source_target_pairs={{1,0},{2,1},{3,2},{4,3},{5,4},{6,5},{7,6},{8,7},{9,8},{10,9},{11,1... | collective-permute-start | bytes 838664 | tf_op jit(solution)/shard_map/ppermute | solution.py:20
  36.6 14.5 %collective-permute-start.2 = (bf16[42,13,256]{2,1,0:T(8,128)(2,1)S(1)}, bf16[42,13,256]{2,1,0:T(8,128)(2,1)S(1)}, u32[]{:S(2)}, u32[]{:S(2)}) collective-permute-start(bf16[42,13,256]{2,1,0:T(8,128)(2,1)S(1)} %get-tuple-element.284), channel_id=1, source_target_pairs={{0,1},{1,2},{2,3},{3,4},{4,5},{5,6},{6,7},{7,8},{8,9},{9,10},{10,1... | collective-permute-start | bytes 838664 | tf_op jit(solution)/shard_map/ppermute | solution.py:17
  38.5 14.5 %collective-permute-start.3 = (bf16[42,13,256]{2,1,0:T(8,128)(2,1)S(1)}, bf16[42,13,256]{2,1,0:T(8,128)(2,1)S(1)}, u32[]{:S(2)}, u32[]{:S(2)}) collective-permute-start(bf16[42,13,256]{2,1,0:T(8,128)(2,1)S(1)} %get-tuple-element.285), channel_id=1, source_target_pairs={{1,0},{2,1},{3,2},{4,3},{5,4},{6,5},{7,6},{8,7},{9,8},{10,9},{11,1... | collective-permute-start | bytes 838664 | tf_op jit(solution)/shard_map/ppermute | solution.py:20
  725.3 2.4 copy-start.3
  726.7 1.9 copy-start.1
Sparse Core Ops, SparseCore 0:
  233.1 492.1 all-reduce.2
where the time goes:
time: 740 us; the launch traced here: 736 us
  waiting for transfers between devices  498 us (67%)
  other arithmetic  110 us (15%)
  local copies, waits for them, and re-layouts  77.1 us (10%)
  starting transfers between devices  30.7 us (4%)
  between operations  14.3 us (2%)
    psum x1, waiting for transfers between devices, per_device(): lax.psum((sum_in, sum_out, kernel_sums), ('row', 'col'))  492 us
    add x27, other arithmetic, sweep(): accumulated = accumulated + tap_row[offset] * shifted  56.6 us
    slice x54, local copies, waits for them, and re-layouts, sweep(): accumulated = accumulated + tap_row[offset] * shifted  55.3 us
    reduce_sum x54, other arithmetic, sweep(): jnp.sum(source_rows[:, offset:offset + tile_cols].astype(jnp.float32) * g...  47.9 us
    ppermute x4, starting transfers between devices, padded_2(): lax.ppermute(lax.slice_in_dim(block, 0, width, axis=dim), axis, backward)  18 us
    dynamic_update_slice x27, local copies, waits for them, and re-layouts, sweep(): lax.dynamic_update_index_in_dim(kernel_sums, jnp.stack(tap_sums), row_off...  16.5 us
  transfers between devices with their start and end apart: 9, of which 3 were waited for; matrix products, arithmetic and copies ran while one was open for 1% of the time, Pallas kernels for 0%

commit v1 on v0

--- a/solution.py
+++ b/solution.py
@@ -1,12 +1,22 @@
+import functools
 import math
 import jax
 import jax.numpy as jnp
 from jax import lax
 from jax.sharding import PartitionSpec as P
+from jax.lax import psum
 
 KS = 27
 gelu_coef = 0.044715
 root_coef = math.sqrt(2.0 / math.pi)
+
+
+def wait_the_chunk(unit, peer_axis, mesh_dim):
+    work_now = psum(unit, peer_axis)
+    return psum(work_now, mesh_dim)
+
+
+feed_the_results = functools.partial(wait_the_chunk, peer_axis="row", mesh_dim="col")
 
 
 def padded_2(block, sides, width):
@@ -82,7 +92,7 @@
     devices_all = lax.axis_size("row") * lax.axis_size("col")
     pixel_count = tile_rows * tile_cols * devices_all
     grad_scale = 1.0 / math.sqrt(pixel_count)
-    total_in, total_out, total_kernel = lax.psum((sum_in, sum_out, kernel_sums), ("row", "col"))
+    total_in, total_out, total_kernel = feed_the_results((sum_in, sum_out, kernel_sums))
     final_in = (total_in * grad_scale).astype(jnp.bfloat16)
     final_out = (total_out * grad_scale).astype(jnp.bfloat16)
     final_kernel = (total_kernel * grad_scale).astype(jnp.bfloat16)

time: 740 us -> 684 us (0.924)
  the two profiles are of different devices: /device:TPU:8 before, /device:TPU:2 now
where the time goes in v1:
time: 684 us; the launch traced here: 680 us
  waiting for transfers between devices  450 us (66%)
  other arithmetic  110 us (16%)
  local copies, waits for them, and re-layouts  77.1 us (11%)
  starting transfers between devices  22.5 us (3%)
  between operations  14.3 us (2%)
    psum x1, waiting for transfers between devices, wait_the_chunk(): return psum(work_now, mesh_dim)  277 us
    psum x1, waiting for transfers between devices, wait_the_chunk(): work_now = psum(unit, peer_axis)  164 us
    add x27, other arithmetic, sweep(): accumulated = accumulated + tap_row[offset] * shifted  56.6 us
    slice x54, local copies, waits for them, and re-layouts, sweep(): accumulated = accumulated + tap_row[offset] * shifted  55.3 us
    reduce_sum x54, other arithmetic, sweep(): jnp.sum(source_rows[:, offset:offset + tile_cols].astype(jnp.float32) * g...  47.9 us
    dynamic_update_slice x27, local copies, waits for them, and re-layouts, sweep(): lax.dynamic_update_index_in_dim(kernel_sums, jnp.stack(tap_sums), row_off...  16.5 us
  transfers between devices with their start and end apart: 10, of which 5 were waited for; matrix products, arithmetic and copies ran while one was open for 1% of the time, Pallas kernels for 0%

profile of v1, /device:TPU:2, one launch (start us, length us, event | category | flops | bytes accessed | tf_op | source)
XLA Modules:
  0.0 680.1 jit_solution(1632951990375004131)
XLA Ops:
  10.2 2.4 collective-permute-start.4
  15.0 7.4 %collective-permute-start.1 = (bf16[13,16,256]{2,1,0:T(8,128)(2,1)S(1)}, bf16[13,16,256]{2,1,0:T(8,128)(2,1)S(1)}, u32[]{:S(2)}, u32[]{:S(2)}) collective-permute-start(bf16[13,16,256]{2,1,0:T(8,128)(2,1)S(1)} %bitcast.191), channel_id=1, source_target_pairs={{32,0},{64,32},{96,64},{128,96},{160,128},{192,160},{224,192},{256... | collective-permute-start | bytes 319496 | tf_op jit(solution)/shard_map/ppermute | solution.py:30
  30.3 4.6 collective-permute-start.2
  37.6 4.0 collective-permute-done.7
  43.5 4.3 collective-permute-done.3
  48.2 179.6 %while.18 = (s32[]{:T(128)}, f32[16,16,256]{2,1,0:T(8,128)S(1)}, f32[27,27,256]{2,1,0:T(8,128)}, f32[27,27,256]{2,1,0:T(8,128)}, bf16[42,42,256]{2,1,0:T(8,128)(...) while((s32[]{:T(128)}, f32[16,16,256]{2,1,0:T(8,128)S(1)}, ...), condition=%wide.region_28.29_spmd.clone, body=%wide.region_0.28_spmd.clone.sunk | while | flops 10806561 | bytes 8091653 | solution.py:90
  52.2 2.1 multiply_add_fusion.3
  58.9 2.1 multiply_add_fusion.3
  65.5 2.1 multiply_add_fusion.3
  72.3 2.1 multiply_add_fusion.3
  78.9 2.1 multiply_add_fusion.3
  85.6 2.1 multiply_add_fusion.3
  98.9 2.1 multiply_add_fusion.3
  105.5 2.1 multiply_add_fusion.3
  112.1 2.1 multiply_add_fusion.3
  118.8 2.1 multiply_add_fusion.3
  125.4 2.1 multiply_add_fusion.3
  132.1 2.1 multiply_add_fusion.3
  138.7 2.1 multiply_add_fusion.3
  145.3 2.1 multiply_add_fusion.3
  152.0 2.1 multiply_add_fusion.3
  165.3 2.1 multiply_add_fusion.3
  171.9 2.1 multiply_add_fusion.3
  178.6 2.1 multiply_add_fusion.3
  185.2 2.1 multiply_add_fusion.3
  191.9 2.1 multiply_add_fusion.3
  198.5 2.1 multiply_add_fusion.3
  205.2 2.1 multiply_add_fusion.3
  218.4 2.1 multiply_add_fusion.3
  225.1 2.1 multiply_add_fusion.3
  227.9 163.8 %all-reduce.7.cloned.1.call-done = (f32[256,1024]{0,1:T(8,128)}, f32[1024,256]{1,0:T(8,128)}, f32[27,27,256]{2,1,0:T(8,128)}) async-done(((f32[256,1024]{0,1:T(8,128)}, f32[1024,256]{1,0:T(8,128)}, f32[27,27,256]{2,1,0:T(8,128)}), (f32[256,1024]{0,1:T(8,128)}, f32[1024,256]{1,0:T(8,128)}, f32[27,27,256]{2,1,0:T(8,128)})) %all-reduce.7.cloned.1.call-update) | async-done | bytes 2843664 | tf_op jit(solution)/shard_map/psum | solution.py:15
  392.3 276.8 %all-reduce.5.cloned.1.call-done = (f32[256,1024]{0,1:T(8,128)}, f32[1024,256]{1,0:T(8,128)}, f32[27,27,256]{2,1,0:T(8,128)}) async-done(((f32[256,1024]{0,1:T(8,128)}, f32[1024,256]{1,0:T(8,128)}, f32[27,27,256]{2,1,0:T(8,128)}), (f32[256,1024]{0,1:T(8,128)}, f32[1024,256]{1,0:T(8,128)}, f32[27,27,256]{2,1,0:T(8,128)})) %all-reduce.5.cloned.1.call-update) | async-done | bytes 2843664 | tf_op jit(solution)/shard_map/psum | solution.py:16
  (219 shorter events, 151.9 us)
Async XLA Ops:
  7.2 5.5 copy-start
  7.2 6.7 copy-start.7
  7.2 6.7 copy-start.6
  7.2 384.4 %all-reduce.7.cloned.1.call-start = ((), (), s32[]{:S(2)}) async-start(), calls=%async_computation.1 | async-start | bytes 5963776 | tf_op jit(solution)/shard_map/psum | solution.py:15
  8.3 18.9 %collective-permute-start.5 = (bf16[13,16,256]{2,1,0:T(8,128)(2,1)S(1)}, bf16[13,16,256]{2,1,0:T(8,128)(2,1)S(1)}, u32[]{:S(2)}, u32[]{:S(2)}) collective-permute-start(bf16[13,16,256]{2,1,0:T(8,128)(2,1)S(1)} %get-tuple-element.289), channel_id=1, source_target_pairs={{32,0},{64,32},{96,64},{128,96},{160,128},{192,160},{224,192},{256... | collective-permute-start | bytes 319496 | tf_op jit(solution)/shard_map/ppermute | solution.py:30
  10.2 16.9 %collective-permute-start.4 = (bf16[13,16,256]{2,1,0:T(8,128)(2,1)S(1)}, bf16[13,16,256]{2,1,0:T(8,128)(2,1)S(1)}, u32[]{:S(2)}, u32[]{:S(2)}) collective-permute-start(bf16[13,16,256]{2,1,0:T(8,128)(2,1)S(1)} %get-tuple-element.290), channel_id=1, source_target_pairs={{0,32},{32,64},{64,96},{96,128},{128,160},{160,192},{192,224},{224... | collective-permute-start | bytes 319496 | tf_op jit(solution)/shard_map/ppermute | solution.py:27
  15.0 15.1 %collective-permute-start.1 = (bf16[13,16,256]{2,1,0:T(8,128)(2,1)S(1)}, bf16[13,16,256]{2,1,0:T(8,128)(2,1)S(1)}, u32[]{:S(2)}, u32[]{:S(2)}) collective-permute-start(bf16[13,16,256]{2,1,0:T(8,128)(2,1)S(1)} %bitcast.191), channel_id=1, source_target_pairs={{32,0},{64,32},{96,64},{128,96},{160,128},{192,160},{224,192},{256... | collective-permute-start | bytes 319496 | tf_op jit(solution)/shard_map/ppermute | solution.py:30
  22.5 3.7 copy-start.5
  22.5 7.7 %collective-permute-start = (bf16[13,16,256]{2,1,0:T(8,128)(2,1)S(1)}, bf16[13,16,256]{2,1,0:T(8,128)(2,1)S(1)}, u32[]{:S(2)}, u32[]{:S(2)}) collective-permute-start(bf16[13,16,256]{2,1,0:T(8,128)(2,1)S(1)} %bitcast.190), channel_id=1, source_target_pairs={{0,32},{32,64},{64,96},{96,128},{128,160},{160,192},{192,224},{224... | collective-permute-start | bytes 319496 | tf_op jit(solution)/shard_map/ppermute | solution.py:27
  26.1 1.0 copy-start.2
  27.4 8.9 %copy-start.4 = (bf16[16,16,256]{2,1,0:T(8,128)(2,1)S(1)}, bf16[16,16,256]{2,1,0:T(8,128)(2,1)}, u32[]{:S(2)}) copy-start(bf16[16,16,256]{2,1,0:T(8,128)(2,1)} %param.9) | copy-start | bytes 393220
  27.4 10.2 %collective-permute-start.6 = (bf16[42,13,256]{2,1,0:T(8,128)(2,1)S(1)}, bf16[42,13,256]{2,1,0:T(8,128)(2,1)S(1)}, u32[]{:S(2)}, u32[]{:S(2)}) collective-permute-start(bf16[42,13,256]{2,1,0:T(8,128)(2,1)S(1)} %get-tuple-element.285), channel_id=1, source_target_pairs={{0,1},{1,2},{2,3},{3,4},{4,5},{5,6},{6,7},{7,8},{8,9},{9,10},{10,1... | collective-permute-start | bytes 838664 | tf_op jit(solution)/shard_map/ppermute | solution.py:27
  28.8 12.8 %collective-permute-start.7 = (bf16[42,13,256]{2,1,0:T(8,128)(2,1)S(1)}, bf16[42,13,256]{2,1,0:T(8,128)(2,1)S(1)}, u32[]{:S(2)}, u32[]{:S(2)}) collective-permute-start(bf16[42,13,256]{2,1,0:T(8,128)(2,1)S(1)} %get-tuple-element.286), channel_id=1, source_target_pairs={{1,0},{2,1},{3,2},{4,3},{5,4},{6,5},{7,6},{8,7},{9,8},{10,9},{11,1... | collective-permute-start | bytes 838664 | tf_op jit(solution)/shard_map/ppermute | solution.py:30
  30.3 13.2 %collective-permute-start.2 = (bf16[42,13,256]{2,1,0:T(8,128)(2,1)S(1)}, bf16[42,13,256]{2,1,0:T(8,128)(2,1)S(1)}, u32[]{:S(2)}, u32[]{:S(2)}) collective-permute-start(bf16[42,13,256]{2,1,0:T(8,128)(2,1)S(1)} %get-tuple-element.287), channel_id=1, source_target_pairs={{0,1},{1,2},{2,3},{3,4},{4,5},{5,6},{6,7},{7,8},{8,9},{9,10},{10,1... | collective-permute-start | bytes 838664 | tf_op jit(solution)/shard_map/ppermute | solution.py:27
  34.9 12.9 %collective-permute-start.3 = (bf16[42,13,256]{2,1,0:T(8,128)(2,1)S(1)}, bf16[42,13,256]{2,1,0:T(8,128)(2,1)S(1)}, u32[]{:S(2)}, u32[]{:S(2)}) collective-permute-start(bf16[42,13,256]{2,1,0:T(8,128)(2,1)S(1)} %get-tuple-element.288), channel_id=1, source_target_pairs={{1,0},{2,1},{3,2},{4,3},{5,4},{6,5},{7,6},{8,7},{9,8},{10,9},{11,1... | collective-permute-start | bytes 838664 | tf_op jit(solution)/shard_map/ppermute | solution.py:30
  227.8 441.3 %all-reduce.5.cloned.1.call-start = ((), (), s32[]{:S(2)}) async-start(), calls=%async_computation | async-start | bytes 5963776 | tf_op jit(solution)/shard_map/psum | solution.py:16
  669.1 2.4 copy-start.3
  670.5 1.9 copy-start.1
Sparse Core Ops, SparseCore 0:
  227.9 163.6 all-reduce.6
  394.8 274.2 all-reduce.4
